TPU v7x, 128 devices: a whole 4x4x4 slice. The times are simulated.
128 devices in a mesh: ctx: 16 (over x, y_hi, core), tp: 8 (over y_lo, z).
Axes of the slice: x: 4, y: 4 (y_hi: 2, y_lo: 2; y = y_hi * 2 + y_lo), z: 4, core: 2. Of those that a mesh axis runs over, the one named last changes fastest.
Arguments:
- queries: bfloat16 [4096, 8192], P('ctx', 'tp'), may hold values from -120 to 120
- key_proj: bfloat16 [4096, 1024], P('ctx', 'tp'), may hold values from -4 to 4
- value_proj: bfloat16 [4096, 1024], P('ctx', 'tp'), may hold values from -6 to 6
- out_weight: bfloat16 [8192, 8192], P('tp'), may hold values from -0.75 to 0.75
- doc_ids: int32 [4096], replicated, may hold values from 0 to 7, never falling along the last dimension, each value on 1 to 2048 neighbouring positions
- drop_seed: int32 [1], replicated, may hold values from 0 to 1073741823
Outputs:
- output: bfloat16 [4096, 8192], P('ctx', 'tp')
Inputs may be any that keep to these rules, and one draw needn't show every extreme that they name: doc_ids never fall along the sequence; each document has 1 to 2048 tokens, one exactly 2048.
All inputs are finite; a program needn't handle non-finite values.
Results may differ from a plain program's by a relative error of at most 0.019.
Values may be sent and summed in bfloat16 or wider, within the bound.
No kernel may reach another device: no remote copies, remote signals or barrier semaphores. Data moves between devices by JAX's collectives and lax.ppermute only.
A program may use at most 128 MiB of HBM per device.

v0:
```python
import math
import jax
import jax.numpy as jnp
from jax import lax
from jax.sharding import PartitionSpec as P

HEADS = 64
KVH = 8
HD = 128


def mixing(value):
    value = value ^ lax.shift_right_logical(value, jnp.int32(16))
    value = value * 73244475
    value = value ^ lax.shift_right_logical(value, jnp.int32(16))
    value = value * 73244475
    value = value ^ lax.shift_right_logical(value, jnp.int32(16))
    return value


def attend_tile(state, context, k_block, v_block, k_start):
    q_heads, q_pos, q_doc, q_hash, doc_ids = context
    count = k_block.shape[0]
    local_kv = q_heads.shape[1]
    k_pos = k_start + jnp.arange(count, dtype=jnp.int32)
    k_doc = lax.dynamic_slice_in_dim(doc_ids, k_start, count)
    peak, row_sum, accum = state
    k_heads = k_block.reshape(count, local_kv, HD)
    v_heads = v_block.reshape(count, local_kv, HD)
    scores = jnp.einsum(
        "qkgd,nkd->qkgn", q_heads, k_heads, preferred_element_type=jnp.float32
    ) * HD ** (-0.5)
    allowed = (q_doc[:, None] == k_doc[None, :]) & (k_pos[None, :] <= q_pos[:, None])
    allowed = allowed[:, None, None, :]
    row_max = jnp.max(jnp.where(allowed, scores, jnp.float32(-1e30)), axis=-1)
    new_peak = jnp.maximum(peak, row_max)
    rescale = jnp.exp(peak - new_peak)
    weights = jnp.where(allowed, jnp.exp(scores - new_peak[..., None]), jnp.float32(0.0))
    row_sum = row_sum * rescale + jnp.sum(weights, axis=-1)
    full_hash = mixing(q_hash + k_pos.reshape(1, 1, 1, count))
    keeper = lax.shift_right_logical(full_hash, jnp.int32(8)) >= 1677722
    dropped = jnp.where(keeper, weights * jnp.float32(1.0 / 0.9), jnp.float32(0.0)).astype(
        jnp.bfloat16
    )
    accum = accum * rescale[..., None] + jnp.einsum(
        "qkgn,nkd->qkgd", dropped, v_heads, preferred_element_type=jnp.float32
    )
    return (new_peak, row_sum, accum)


def attend_range(state, context, k_rows, v_rows):
    count = k_rows.shape[0]
    tile_rows = math.gcd(count, 512)

    def step_tile(number, current):
        offset = number * tile_rows
        k_tile = lax.dynamic_slice_in_dim(k_rows, offset, tile_rows, 0)
        v_tile = lax.dynamic_slice_in_dim(v_rows, offset, tile_rows, 0)
        return attend_tile(current, context, k_tile, v_tile, offset)

    return lax.fori_loop(0, count // tile_rows, step_tile, state)


def body(queries, key_proj, value_proj, out_weight, doc_ids, drop_seed):
    tok_rows = queries.shape[0]
    half_rows = tok_rows // 2
    local_kv = key_proj.shape[1] // HD
    per_group = HEADS // KVH
    ctx_index = lax.axis_index("ctx")
    tp_index = lax.axis_index("tp")
    head_ids = tp_index * (local_kv * per_group) + jnp.arange(local_kv * per_group, dtype=jnp.int32)
    head_ids = head_ids.reshape(1, local_kv, per_group, 1)
    seed_value = drop_seed[0]
    half_index = jnp.arange(half_rows, dtype=jnp.int32)
    first_q = queries[:half_rows]
    second_q = queries[half_rows:]
    first_pos = ctx_index * tok_rows + half_index
    second_pos = ctx_index * tok_rows + half_rows + half_index
    contexts = []
    for half_q, half_pos in ((first_q, first_pos), (second_q, second_pos)):
        q_heads = half_q.reshape(half_rows, local_kv, per_group, HD)
        q_doc = lax.dynamic_slice_in_dim(doc_ids, half_pos[0], half_rows)
        q_hash = mixing(
            mixing(seed_value * 7919 + head_ids) ^ half_pos.reshape(half_rows, 1, 1, 1) * 65537
        )
        contexts.append((q_heads, half_pos, q_doc, q_hash, doc_ids))

    def start_state():
        return (
            jnp.full((half_rows, local_kv, per_group), -1e30, jnp.float32),
            jnp.zeros((half_rows, local_kv, per_group), jnp.float32),
            jnp.zeros((half_rows, local_kv, per_group, HD), jnp.float32),
        )

    piece = (
        lax.all_gather(key_proj, "ctx", axis=0, tiled=True),
        lax.all_gather(value_proj, "ctx", axis=0, tiled=True),
    )
    final = (
        attend_range(start_state(), contexts[0], piece[0], piece[1]),
        attend_range(start_state(), contexts[1], piece[0], piece[1]),
    )
    halves = []
    for state in final:
        peak, row_sum, accum = state
        halves.append(
            (accum / row_sum[..., None])
            .astype(jnp.bfloat16)
            .reshape(half_rows, local_kv * per_group * HD)
        )
    second_rows = halves[1]
    attention = jnp.concatenate([halves[0], second_rows], axis=0)
    partial_value = jnp.dot(attention, out_weight, preferred_element_type=jnp.float32)
    return lax.psum_scatter(
        partial_value.astype(jnp.bfloat16), "tp", scatter_dimension=1, tiled=True
    )


def solution(mesh):
    in_specs = (P("ctx", "tp"), P("ctx", "tp"), P("ctx", "tp"), P("tp", None), P(), P())
    out_specs = P("ctx", "tp")
    return jax.shard_map(body, mesh=mesh, in_specs=in_specs, out_specs=out_specs, check_vma=False)
```

profile of v0, /device:TPU:1, one launch (start us, length us, event | category | flops | bytes accessed | tf_op | source)
XLA Modules:
  0.0 272.1 jit_solution(3087980518251727780)
XLA Ops:
  7.3 1.6 copy.13
  12.6 45.7 %all-gather.3.cloned.1.call-done = bf16[4096,128]{1,0:T(8,128)(2,1)} async-done(((bf16[256,128]{1,0:T(8,128)(2,1)}), bf16[4096,128]{1,0:T(8,128)(2,1)}) %all-gather.3.cloned.1.call-update) | async-done | bytes 1048592 | tf_op jit(solution)/shard_map/all_gather | solution.py:96
  58.4 46.4 %all-gather.5.cloned.1.call-done = bf16[4096,128]{0,1:T(8,128)(2,1)} async-done(((bf16[256,128]{0,1:T(8,128)(2,1)}), bf16[4096,128]{0,1:T(8,128)(2,1)}) %all-gather.5.cloned.1.call-update) | async-done | bytes 1048592 | tf_op jit(solution)/shard_map/all_gather | solution.py:97
  104.7 53.2 %while.37 = (s32[]{:T(128)}, f32[128,1,8]{0,2,1:T(8,128)S(1)}, f32[128,1,8]{0,2,1:T(8,128)S(1)}, f32[128,1,8,128]{0,3,2,1:T(8,128)}, s32[128]{0:T(128)S(1)}, /*i...) while((s32[]{:T(128)}, f32[128,1,8]{0,2,1:T(8,128)S(1)}, ...), condition=%wide.region_7.8_spmd.clone, body=%wide.region_4.7_spmd.clone.sunk | while | flops 281624192 | bytes 12409155 | solution.py:61
  108.1 2.4 fusion.104
  112.4 1.4 fusion.100
  114.8 2.4 fusion.104
  121.4 2.4 fusion.104
  125.7 1.4 fusion.100
  128.1 2.4 fusion.104
  134.7 2.4 fusion.104
  139.0 1.4 fusion.100
  141.4 2.4 fusion.104
  148.0 2.4 fusion.104
  152.3 1.4 fusion.100
  154.7 2.4 fusion.104
  157.9 43.4 %while.36 = (s32[]{:T(128)}, f32[128,1,8]{0,2,1:T(8,128)S(1)}, f32[128,1,8]{0,2,1:T(8,128)S(1)}, f32[128,1,8,128]{0,3,2,1:T(8,128)S(1)}, s32[128]{0:T(128)S(1)},...) while((s32[]{:T(128)}, f32[128,1,8]{0,2,1:T(8,128)S(1)}, ...), condition=%wide.region_3.4_spmd.clone, body=%wide.region_0.3_spmd.clone.sunk | while | flops 281624192 | bytes 8214795 | solution.py:61
  159.0 1.4 fusion.93
  160.9 2.4 fusion.97
  164.4 1.4 fusion.93
  166.4 2.4 fusion.97
  169.8 1.4 fusion.93
  171.8 2.4 fusion.97
  177.2 2.4 fusion.97
  182.6 2.4 fusion.97
  186.1 1.4 fusion.93
  188.0 2.4 fusion.97
  191.5 1.4 fusion.93
  193.5 2.4 fusion.97
  198.9 2.4 fusion.97
  201.5 12.1 %convolution_convert_fusion = bf16[256,8192]{1,0:T(8,128)(2,1)} fusion(bf16[1024,8192]{1,0:T(8,128)(2,1)} %param.13, bf16[128,1024]{0,1:T(8,128)(2,1)S(1)} %bitcast.164, bf16[128,1024]{0,1:T(8,128)(2,1)S(1)} %bitcast.165), kind=kOutput, calls=%fused_computation.100 | convolution fusion | flops 4298113024 | bytes 21495808 | tf_op jit(solution)/shard_map/dot_general | solution.py:113
  213.6 51.9 %reduce-scatter.2.cloned.1.call-done = bf16[256,1024]{1,0:T(8,128)(2,1)} async-done(((bf16[256,8192]{1,0:T(8,128)(2,1)}), bf16[256,1024]{1,0:T(8,128)(2,1)}) %reduce-scatter.2.cloned.1.call-update) | async-done | bytes 524304 | tf_op jit(solution)/shard_map/reduce_scatter | solution.py:114
  (209 shorter events, 47.5 us)
Async XLA Ops:
  6.5 51.8 %all-gather.3.cloned.1.call-start = ((), (), s32[]{:S(2)}) async-start(), calls=%async_computation.1 | async-start | bytes 1114112 | tf_op jit(solution)/shard_map/all_gather | solution.py:96
  7.3 97.5 %all-gather.5.cloned.1.call-start = ((), (), s32[]{:S(2)}) async-start(), calls=%async_computation.2 | async-start | bytes 1114112 | tf_op jit(solution)/shard_map/all_gather | solution.py:97
  8.9 256.6 %reduce-scatter.2.cloned.1.call-start = ((), (), s32[]{:S(2)}) async-start(), calls=%async_computation.3 | async-start | bytes 4718592 | tf_op jit(solution)/shard_map/reduce_scatter | solution.py:114
  107.1 1.0 copy-start
  110.6 0.8 copy-start.1
  113.8 1.0 copy-start
  117.2 0.8 copy-start.1
  120.4 1.0 copy-start
  123.9 0.8 copy-start.1
  127.0 1.0 copy-start
  130.5 0.8 copy-start.1
  133.7 1.0 copy-start
  137.2 0.8 copy-start.1
  140.3 1.0 copy-start
  143.8 0.8 copy-start.1
  147.0 1.0 copy-start
  150.5 0.8 copy-start.1
  153.6 1.0 copy-start
  157.1 0.8 copy-start.1
  157.9 43.4 %copy-start.2 = (f32[128,1,8,128]{0,3,2,1:T(8,128)S(1)}, f32[128,1,8,128]{0,3,2,1:T(8,128)}, u32[]{:S(2)}) copy-start(f32[128,1,8,128]{0,3,2,1:T(8,128)} %get-tuple-element.377) | copy-start | bytes 1572868
Sparse Core Ops, SparseCore 0:
  9.8 48.5 all-gather.2
  60.6 44.0 all-gather.4
  213.7 51.7 reduce-scatter.1
where the time goes:
time: 274 us; the launch traced here: 272 us
  waiting for transfers between devices  145 us (53%)
  matrix products  73.1 us (27%)
  local copies, waits for them, and re-layouts  25.6 us (9%)
  between operations  14.1 us (5%)
  other arithmetic  13 us (5%)
    reduce_scatter x1, waiting for transfers between devices, body(): lax.psum_scatter(partial_value.astype(jnp.bfloat16), 'tp', scatter_dimens...  51.9 us
    all_gather x1, waiting for transfers between devices, body(): lax.all_gather(value_proj, 'ctx', axis=0, tiled=True)  46.4 us
    all_gather x1, waiting for transfers between devices, body(): lax.all_gather(key_proj, 'ctx', axis=0, tiled=True)  45.7 us
    dot_general x16, matrix products, attend_tile(): jnp.einsum('qkgn,nkd->qkgd', dropped, v_heads, preferred_element_type=jnp...  39.1 us
    dot_general x16, matrix products, attend_tile(): jnp.einsum('qkgd,nkd->qkgn', q_heads, k_heads, preferred_element_type=jnp...  21.9 us
    dynamic_slice x16, local copies, waits for them, and re-layouts, attend_tile(): k_doc = lax.dynamic_slice_in_dim(doc_ids, k_start, count)  12.2 us
    dot_general x1, matrix products, body(): jnp.dot(attention, out_weight, preferred_element_type=jnp.float32)  12.1 us
    while x48, local copies, waits for them, and re-layouts  10.1 us
  transfers between devices with their start and end apart: 3, of which 3 were waited for; matrix products, arithmetic and copies ran while one was open for 2% of the time, Pallas kernels for 0%

commit v1 on v0

--- a/solution.py
+++ b/solution.py
@@ -1,12 +1,30 @@
+import functools
 import math
 import jax
 import jax.numpy as jnp
 from jax import lax
 from jax.sharding import PartitionSpec as P
+from jax.lax import all_to_all, axis_size
 
 HEADS = 64
 KVH = 8
 HD = 128
+
+
+def find_group(mine, device_axis):
+    all_values = jnp.concatenate(
+        all_to_all(
+            jnp.stack([mine] * axis_size(device_axis)),
+            axis_name=device_axis,
+            concat_axis=0,
+            split_axis=0,
+        ),
+        axis=0,
+    )
+    return all_values
+
+
+_mark_targets = functools.partial(find_group, device_axis="ctx")
 
 
 def mixing(value):
@@ -92,10 +110,7 @@
             jnp.zeros((half_rows, local_kv, per_group, HD), jnp.float32),
         )
 
-    piece = (
-        lax.all_gather(key_proj, "ctx", axis=0, tiled=True),
-        lax.all_gather(value_proj, "ctx", axis=0, tiled=True),
-    )
+    piece = (lax.all_gather(key_proj, "ctx", axis=0, tiled=True), _mark_targets(value_proj))
     final = (
         attend_range(start_state(), contexts[0], piece[0], piece[1]),
         attend_range(start_state(), contexts[1], piece[0], piece[1]),

time: 274 us -> 228 us (0.83)
  waiting for transfers between devices: 145 us -> 91.9 us
  starting transfers between devices: 0.08 us -> 8.49 us
  local copies, waits for them, and re-layouts: 25.6 us -> 18 us
  matrix products: 73.1 us -> 80.1 us
    all_gather x1 -> x0, waiting for transfers between devices: 46.4 us -> none  [body(): lax.all_gather(value_proj, 'ctx', axis=0, tiled=True)]
    all_gather x1, waiting for transfers between devices: 45.7 us -> 24 us  [body(): lax.all_gather(key_proj, 'ctx', axis=0, tiled=True)]
    all_to_all x0 -> x1, waiting for transfers between devices: none -> 15.3 us  [find_group(): all_to_all(jnp.stack([mine] * axis_size(device_axis)), axis_name=device_a...]
    while x48 -> x16, local copies, waits for them, and re-layouts: 10.1 us -> 0.04 us
    all_to_all x0 -> x1, starting transfers between devices: none -> 8.45 us  [find_group(): all_to_all(jnp.stack([mine] * axis_size(device_axis)), axis_name=device_a...]
    dot_general x16, matrix products: 39.1 us -> 46.2 us  [attend_tile(): jnp.einsum('qkgn,nkd->qkgd', dropped, v_heads, preferred_element_type=jnp...]
  transfers between devices with their start and end apart: 3 -> 3, of which waited for: 3 -> 3; matrix products, arithmetic and copies ran while one was open for 2% -> 3% of each run, Pallas kernels for 0% -> 0%
where the time goes in v1:
time: 228 us; the launch traced here: 226 us
  waiting for transfers between devices  91.9 us (40%)
  matrix products  80.1 us (35%)
  local copies, waits for them, and re-layouts  18 us (8%)
  between operations  14.5 us (6%)
  other arithmetic  12.1 us (5%)
  starting transfers between devices  8.49 us (4%)
    reduce_scatter x1, waiting for transfers between devices, body(): lax.psum_scatter(partial_value.astype(jnp.bfloat16), 'tp', scatter_dimens...  51.9 us
    dot_general x16, matrix products, attend_tile(): jnp.einsum('qkgn,nkd->qkgd', dropped, v_heads, preferred_element_type=jnp...  46.2 us
    all_gather x1, waiting for transfers between devices, body(): lax.all_gather(key_proj, 'ctx', axis=0, tiled=True)  24 us
    dot_general x16, matrix products, attend_tile(): jnp.einsum('qkgd,nkd->qkgn', q_heads, k_heads, preferred_element_type=jnp...  21.8 us
    all_to_all x1, waiting for transfers between devices, find_group(): all_to_all(jnp.stack([mine] * axis_size(device_axis)), axis_name=device_a...  15.3 us
    dynamic_slice x16, local copies, waits for them, and re-layouts, attend_tile(): k_doc = lax.dynamic_slice_in_dim(doc_ids, k_start, count)  12.3 us
    dot_general x1, matrix products, body(): jnp.dot(attention, out_weight, preferred_element_type=jnp.float32)  12.1 us
    all_to_all x1, starting transfers between devices, find_group(): all_to_all(jnp.stack([mine] * axis_size(device_axis)), axis_name=device_a...  8.45 us
  transfers between devices with their start and end apart: 3, of which 3 were waited for; matrix products, arithmetic and copies ran while one was open for 3% of the time, Pallas kernels for 0%

profile of v1, /device:TPU:1, one launch (start us, length us, event | category | flops | bytes accessed | tf_op | source)
XLA Modules:
  0.0 226.2 jit_solution(11844304361821582917)
XLA Ops:
  9.3 8.4 %all-to-all-start = ((bf16[16,256,128]{1,2,0:T(8,128)(2,1)}), bf16[16,256,128]{1,2,0:T(8,128)(2,1)S(1)}, u32[]{:S(2)}, u32[]{:S(2)}) async-start(bf16[16,256,128]{1,2,0:T(8,128)(2,1)} %stack.2), calls=%async_computation | async-start | bytes 2097152 | tf_op jit(solution)/shard_map/all_to_all | solution.py:16
  20.5 15.3 %all-to-all-done = bf16[16,256,128]{1,2,0:T(8,128)(2,1)S(1)} async-done(((bf16[16,256,128]{1,2,0:T(8,128)(2,1)}), bf16[16,256,128]{1,2,0:T(8,128)(2,1)S(1)}, u32[]{:S(2)}, u32[]{:S(2)}) %all-to-all-start) | async-done | bytes 1048608 | tf_op jit(solution)/shard_map/all_to_all | solution.py:16
  37.8 24.0 %all-gather.2.cloned.1.call-done = bf16[4096,128]{1,0:T(8,128)(2,1)} async-done(((bf16[256,128]{1,0:T(8,128)(2,1)}), bf16[4096,128]{1,0:T(8,128)(2,1)}) %all-gather.2.cloned.1.call-update) | async-done | bytes 1048592 | tf_op jit(solution)/shard_map/all_gather | solution.py:113
  61.8 50.2 %while.36 = (s32[]{:T(128)}, f32[128,1,8]{0,2,1:T(8,128)S(1)}, f32[128,1,8]{0,2,1:T(8,128)S(1)}, f32[128,1,8,128]{0,3,2,1:T(8,128)}, s32[128]{0:T(128)S(1)}, /*i...) while((s32[]{:T(128)}, f32[128,1,8]{0,2,1:T(8,128)S(1)}, ...), condition=%wide.region_3.4_spmd.clone, body=%wide.region_0.3_spmd.clone.sunk | while | flops 281624192 | bytes 8214787 | solution.py:79
  62.8 1.4 fusion.93
  64.3 3.2 %fusion.97 = f32[128,1,8,128]{0,3,2,1:T(8,128)} fusion(f32[512,128,8]{1,0,2:T(8,128)S(1)} %get-tuple-element.747, s32[512]{0:T(512)S(1)} %iota_add_fusion.11, s32[128,8]{0,1:T(8,128)S(1)} %fusion.96, f32[128,8]{0,1:T(8,128)S(1)} %bitcast.162, pred[128,512]{0,1:T(8,128)(4,1)S(1)} %compare_and_fusion.4, f32[128,1,8,128]{0,3,2,1:T(8,128)} %get-tuple-element.832, ...), kind=kOutput, calls=%fused_computation.19.clone.1 | convolution fusion | flops 143523840 | bytes 3356677 | tf_op jit(solution)/shard_map/while/body/eval_jaxpr/qkgn,nkd->qkgd/dot_general | solution.py:63
  70.3 3.4 %fusion.97 = f32[128,1,8,128]{0,3,2,1:T(8,128)} fusion(f32[512,128,8]{1,0,2:T(8,128)S(1)} %get-tuple-element.747, s32[512]{0:T(512)S(1)} %iota_add_fusion.11, s32[128,8]{0,1:T(8,128)S(1)} %fusion.96, f32[128,8]{0,1:T(8,128)S(1)} %bitcast.162, pred[128,512]{0,1:T(8,128)(4,1)S(1)} %compare_and_fusion.4, f32[128,1,8,128]{0,3,2,1:T(8,128)} %get-tuple-element.832, ...), kind=kOutput, calls=%fused_computation.19.clone.1 | convolution fusion | flops 143523840 | bytes 3356677 | tf_op jit(solution)/shard_map/while/body/eval_jaxpr/qkgn,nkd->qkgd/dot_general | solution.py:63
  75.2 1.4 fusion.93
  76.6 3.4 %fusion.97 = f32[128,1,8,128]{0,3,2,1:T(8,128)} fusion(f32[512,128,8]{1,0,2:T(8,128)S(1)} %get-tuple-element.747, s32[512]{0:T(512)S(1)} %iota_add_fusion.11, s32[128,8]{0,1:T(8,128)S(1)} %fusion.96, f32[128,8]{0,1:T(8,128)S(1)} %bitcast.162, pred[128,512]{0,1:T(8,128)(4,1)S(1)} %compare_and_fusion.4, f32[128,1,8,128]{0,3,2,1:T(8,128)} %get-tuple-element.832, ...), kind=kOutput, calls=%fused_computation.19.clone.1 | convolution fusion | flops 143523840 | bytes 3356677 | tf_op jit(solution)/shard_map/while/body/eval_jaxpr/qkgn,nkd->qkgd/dot_general | solution.py:63
  83.0 3.4 %fusion.97 = f32[128,1,8,128]{0,3,2,1:T(8,128)} fusion(f32[512,128,8]{1,0,2:T(8,128)S(1)} %get-tuple-element.747, s32[512]{0:T(512)S(1)} %iota_add_fusion.11, s32[128,8]{0,1:T(8,128)S(1)} %fusion.96, f32[128,8]{0,1:T(8,128)S(1)} %bitcast.162, pred[128,512]{0,1:T(8,128)(4,1)S(1)} %compare_and_fusion.4, f32[128,1,8,128]{0,3,2,1:T(8,128)} %get-tuple-element.832, ...), kind=kOutput, calls=%fused_computation.19.clone.1 | convolution fusion | flops 143523840 | bytes 3356677 | tf_op jit(solution)/shard_map/while/body/eval_jaxpr/qkgn,nkd->qkgd/dot_general | solution.py:63
  87.8 1.4 fusion.93
  89.3 3.4 %fusion.97 = f32[128,1,8,128]{0,3,2,1:T(8,128)} fusion(f32[512,128,8]{1,0,2:T(8,128)S(1)} %get-tuple-element.747, s32[512]{0:T(512)S(1)} %iota_add_fusion.11, s32[128,8]{0,1:T(8,128)S(1)} %fusion.96, f32[128,8]{0,1:T(8,128)S(1)} %bitcast.162, pred[128,512]{0,1:T(8,128)(4,1)S(1)} %compare_and_fusion.4, f32[128,1,8,128]{0,3,2,1:T(8,128)} %get-tuple-element.832, ...), kind=kOutput, calls=%fused_computation.19.clone.1 | convolution fusion | flops 143523840 | bytes 3356677 | tf_op jit(solution)/shard_map/while/body/eval_jaxpr/qkgn,nkd->qkgd/dot_general | solution.py:63
  95.6 3.4 %fusion.97 = f32[128,1,8,128]{0,3,2,1:T(8,128)} fusion(f32[512,128,8]{1,0,2:T(8,128)S(1)} %get-tuple-element.747, s32[512]{0:T(512)S(1)} %iota_add_fusion.11, s32[128,8]{0,1:T(8,128)S(1)} %fusion.96, f32[128,8]{0,1:T(8,128)S(1)} %bitcast.162, pred[128,512]{0,1:T(8,128)(4,1)S(1)} %compare_and_fusion.4, f32[128,1,8,128]{0,3,2,1:T(8,128)} %get-tuple-element.832, ...), kind=kOutput, calls=%fused_computation.19.clone.1 | convolution fusion | flops 143523840 | bytes 3356677 | tf_op jit(solution)/shard_map/while/body/eval_jaxpr/qkgn,nkd->qkgd/dot_general | solution.py:63
  100.4 1.4 fusion.93
  101.9 3.4 %fusion.97 = f32[128,1,8,128]{0,3,2,1:T(8,128)} fusion(f32[512,128,8]{1,0,2:T(8,128)S(1)} %get-tuple-element.747, s32[512]{0:T(512)S(1)} %iota_add_fusion.11, s32[128,8]{0,1:T(8,128)S(1)} %fusion.96, f32[128,8]{0,1:T(8,128)S(1)} %bitcast.162, pred[128,512]{0,1:T(8,128)(4,1)S(1)} %compare_and_fusion.4, f32[128,1,8,128]{0,3,2,1:T(8,128)} %get-tuple-element.832, ...), kind=kOutput, calls=%fused_computation.19.clone.1 | convolution fusion | flops 143523840 | bytes 3356677 | tf_op jit(solution)/shard_map/while/body/eval_jaxpr/qkgn,nkd->qkgd/dot_general | solution.py:63
  108.2 3.4 %fusion.97 = f32[128,1,8,128]{0,3,2,1:T(8,128)} fusion(f32[512,128,8]{1,0,2:T(8,128)S(1)} %get-tuple-element.747, s32[512]{0:T(512)S(1)} %iota_add_fusion.11, s32[128,8]{0,1:T(8,128)S(1)} %fusion.96, f32[128,8]{0,1:T(8,128)S(1)} %bitcast.162, pred[128,512]{0,1:T(8,128)(4,1)S(1)} %compare_and_fusion.4, f32[128,1,8,128]{0,3,2,1:T(8,128)} %get-tuple-element.832, ...), kind=kOutput, calls=%fused_computation.19.clone.1 | convolution fusion | flops 143523840 | bytes 3356677 | tf_op jit(solution)/shard_map/while/body/eval_jaxpr/qkgn,nkd->qkgd/dot_general | solution.py:63
  112.0 43.2 %while.37 = (s32[]{:T(128)}, f32[128,1,8]{0,2,1:T(8,128)S(1)}, f32[128,1,8]{0,2,1:T(8,128)S(1)}, f32[128,1,8,128]{0,3,2,1:T(8,128)S(1)}, s32[128]{0:T(128)S(1)},...) while((s32[]{:T(128)}, f32[128,1,8]{0,2,1:T(8,128)S(1)}, ...), condition=%wide.region_7.8_spmd.clone, body=%wide.region_4.7_spmd.clone.sunk | while | flops 281624192 | bytes 8214787 | solution.py:79
  113.1 1.4 fusion.100
  114.5 2.4 %fusion.104 = f32[128,1,8,128]{0,3,2,1:T(8,128)S(1)} fusion(f32[512,128,8]{1,0,2:T(8,128)S(1)} %get-tuple-element.763, s32[512]{0:T(512)S(1)} %iota_add_fusion.13, s32[128,8]{0,1:T(8,128)S(1)} %fusion.103, f32[128,8]{0,1:T(8,128)S(1)} %bitcast.164, pred[128,512]{0,1:T(8,128)(4,1)S(1)} %compare_and_fusion.5, ...), kind=kOutput, calls=%fused_computation.67.clone.1 | convolution fusion | flops 143523840 | bytes 3356677 | tf_op jit(solution)/shard_map/while/body/eval_jaxpr/qkgn,nkd->qkgd/dot_general | solution.py:63
  119.9 2.4 %fusion.104 = f32[128,1,8,128]{0,3,2,1:T(8,128)S(1)} fusion(f32[512,128,8]{1,0,2:T(8,128)S(1)} %get-tuple-element.763, s32[512]{0:T(512)S(1)} %iota_add_fusion.13, s32[128,8]{0,1:T(8,128)S(1)} %fusion.103, f32[128,8]{0,1:T(8,128)S(1)} %bitcast.164, pred[128,512]{0,1:T(8,128)(4,1)S(1)} %compare_and_fusion.5, ...), kind=kOutput, calls=%fused_computation.67.clone.1 | convolution fusion | flops 143523840 | bytes 3356677 | tf_op jit(solution)/shard_map/while/body/eval_jaxpr/qkgn,nkd->qkgd/dot_general | solution.py:63
  123.9 1.4 fusion.100
  125.3 2.4 %fusion.104 = f32[128,1,8,128]{0,3,2,1:T(8,128)S(1)} fusion(f32[512,128,8]{1,0,2:T(8,128)S(1)} %get-tuple-element.763, s32[512]{0:T(512)S(1)} %iota_add_fusion.13, s32[128,8]{0,1:T(8,128)S(1)} %fusion.103, f32[128,8]{0,1:T(8,128)S(1)} %bitcast.164, pred[128,512]{0,1:T(8,128)(4,1)S(1)} %compare_and_fusion.5, ...), kind=kOutput, calls=%fused_computation.67.clone.1 | convolution fusion | flops 143523840 | bytes 3356677 | tf_op jit(solution)/shard_map/while/body/eval_jaxpr/qkgn,nkd->qkgd/dot_general | solution.py:63
  130.7 2.4 %fusion.104 = f32[128,1,8,128]{0,3,2,1:T(8,128)S(1)} fusion(f32[512,128,8]{1,0,2:T(8,128)S(1)} %get-tuple-element.763, s32[512]{0:T(512)S(1)} %iota_add_fusion.13, s32[128,8]{0,1:T(8,128)S(1)} %fusion.103, f32[128,8]{0,1:T(8,128)S(1)} %bitcast.164, pred[128,512]{0,1:T(8,128)(4,1)S(1)} %compare_and_fusion.5, ...), kind=kOutput, calls=%fused_computation.67.clone.1 | convolution fusion | flops 143523840 | bytes 3356677 | tf_op jit(solution)/shard_map/while/body/eval_jaxpr/qkgn,nkd->qkgd/dot_general | solution.py:63
  134.6 1.4 fusion.100
  136.1 2.4 %fusion.104 = f32[128,1,8,128]{0,3,2,1:T(8,128)S(1)} fusion(f32[512,128,8]{1,0,2:T(8,128)S(1)} %get-tuple-element.763, s32[512]{0:T(512)S(1)} %iota_add_fusion.13, s32[128,8]{0,1:T(8,128)S(1)} %fusion.103, f32[128,8]{0,1:T(8,128)S(1)} %bitcast.164, pred[128,512]{0,1:T(8,128)(4,1)S(1)} %compare_and_fusion.5, ...), kind=kOutput, calls=%fused_computation.67.clone.1 | convolution fusion | flops 143523840 | bytes 3356677 | tf_op jit(solution)/shard_map/while/body/eval_jaxpr/qkgn,nkd->qkgd/dot_general | solution.py:63
  140.0 1.4 fusion.100
  141.5 2.4 %fusion.104 = f32[128,1,8,128]{0,3,2,1:T(8,128)S(1)} fusion(f32[512,128,8]{1,0,2:T(8,128)S(1)} %get-tuple-element.763, s32[512]{0:T(512)S(1)} %iota_add_fusion.13, s32[128,8]{0,1:T(8,128)S(1)} %fusion.103, f32[128,8]{0,1:T(8,128)S(1)} %bitcast.164, pred[128,512]{0,1:T(8,128)(4,1)S(1)} %compare_and_fusion.5, ...), kind=kOutput, calls=%fused_computation.67.clone.1 | convolution fusion | flops 143523840 | bytes 3356677 | tf_op jit(solution)/shard_map/while/body/eval_jaxpr/qkgn,nkd->qkgd/dot_general | solution.py:63
  146.9 2.4 %fusion.104 = f32[128,1,8,128]{0,3,2,1:T(8,128)S(1)} fusion(f32[512,128,8]{1,0,2:T(8,128)S(1)} %get-tuple-element.763, s32[512]{0:T(512)S(1)} %iota_add_fusion.13, s32[128,8]{0,1:T(8,128)S(1)} %fusion.103, f32[128,8]{0,1:T(8,128)S(1)} %bitcast.164, pred[128,512]{0,1:T(8,128)(4,1)S(1)} %compare_and_fusion.5, ...), kind=kOutput, calls=%fused_computation.67.clone.1 | convolution fusion | flops 143523840 | bytes 3356677 | tf_op jit(solution)/shard_map/while/body/eval_jaxpr/qkgn,nkd->qkgd/dot_general | solution.py:63
  150.8 1.4 fusion.100
  152.3 2.4 %fusion.104 = f32[128,1,8,128]{0,3,2,1:T(8,128)S(1)} fusion(f32[512,128,8]{1,0,2:T(8,128)S(1)} %get-tuple-element.763, s32[512]{0:T(512)S(1)} %iota_add_fusion.13, s32[128,8]{0,1:T(8,128)S(1)} %fusion.103, f32[128,8]{0,1:T(8,128)S(1)} %bitcast.164, pred[128,512]{0,1:T(8,128)(4,1)S(1)} %compare_and_fusion.5, ...), kind=kOutput, calls=%fused_computation.67.clone.1 | convolution fusion | flops 143523840 | bytes 3356677 | tf_op jit(solution)/shard_map/while/body/eval_jaxpr/qkgn,nkd->qkgd/dot_general | solution.py:63
  155.3 12.1 %convolution_convert_fusion = bf16[256,8192]{1,0:T(8,128)(2,1)} fusion(bf16[1024,8192]{1,0:T(8,128)(2,1)} %param.13, bf16[128,1024]{0,1:T(8,128)(2,1)S(1)} %bitcast.167, bf16[128,1024]{0,1:T(8,128)(2,1)S(1)} %bitcast.166), kind=kOutput, calls=%fused_computation.100 | convolution fusion | flops 4298113024 | bytes 21495808 | tf_op jit(solution)/shard_map/dot_general | solution.py:128
  167.5 51.9 %reduce-scatter.2.cloned.1.call-done = bf16[256,1024]{1,0:T(8,128)(2,1)} async-done(((bf16[256,8192]{1,0:T(8,128)(2,1)}), bf16[256,1024]{1,0:T(8,128)(2,1)}) %reduce-scatter.2.cloned.1.call-update) | async-done | bytes 524304 | tf_op jit(solution)/shard_map/reduce_scatter | solution.py:129
  (182 shorter events, 40.4 us)
Async XLA Ops:
  6.5 12.2 %copy-start.1 = (bf16[256,1024]{1,0:T(8,128)(2,1)S(1)}, bf16[256,1024]{1,0:T(8,128)(2,1)}, u32[]{:S(2)}) copy-start(bf16[256,1024]{1,0:T(8,128)(2,1)} %param.10) | copy-start | bytes 1572868
  6.5 55.3 %all-gather.2.cloned.1.call-start = ((), (), s32[]{:S(2)}) async-start(), calls=%async_computation.2 | async-start | bytes 1114112 | tf_op jit(solution)/shard_map/all_gather | solution.py:113
  9.3 26.4 %all-to-all-start = ((bf16[16,256,128]{1,2,0:T(8,128)(2,1)}), bf16[16,256,128]{1,2,0:T(8,128)(2,1)S(1)}, u32[]{:S(2)}, u32[]{:S(2)}) async-start(bf16[16,256,128]{1,2,0:T(8,128)(2,1)} %stack.2), calls=%async_computation | async-start | bytes 2097152 | tf_op jit(solution)/shard_map/all_to_all | solution.py:16
  17.8 201.6 %reduce-scatter.2.cloned.1.call-start = ((), (), s32[]{:S(2)}) async-start(), calls=%async_computation.3 | async-start | bytes 4718592 | tf_op jit(solution)/shard_map/reduce_scatter | solution.py:129
  112.0 43.2 %copy-start = (f32[128,1,8,128]{0,3,2,1:T(8,128)S(1)}, f32[128,1,8,128]{0,3,2,1:T(8,128)}, u32[]{:S(2)}) copy-start(f32[128,1,8,128]{0,3,2,1:T(8,128)} %get-tuple-element.375) | copy-start | bytes 1572868
Sparse Core Ops, SparseCore 0:
  9.8 52.0 all-gather.1
  167.6 51.7 reduce-scatter.1
